TPU v7x, 32 devices: a whole 2x2x4 slice. The times are simulated.
32 devices in a mesh: row: 8 (over z, core), col: 4 (over y, x).
Axes of the slice: x: 2, y: 2, z: 4, core: 2. Of those that a mesh axis runs over, the one named last changes fastest.
Arguments:
- starting_state: float32 [4096, 256], P(('row', 'col')), may hold values from -1 to 1
- features: float32 [4096, 128], P(('row', 'col')), may hold values from -6 to 6
- cotangent: float32 [4096, 256], P(('row', 'col')), may hold values from -6 to 6
- degrees: int32 [4096], P(('row', 'col')), may hold values from 8 to 64
- tile_values: bfloat16 [8, 4, 4, 128, 128], P('row', 'col'), may hold values from 0 to 1, as said below
- tile_rows: int32 [8, 4, 4], P('row', 'col'), may hold values from 0 to 3, as said below
- tile_cols: int32 [8, 4, 4], P('row', 'col'), may hold values from 0 to 7, as said below
- tile_live: int32 [8, 4, 4], P('row', 'col'), may hold values from 0 to 1, as said below
- weight: float32 [256, 256], replicated, may hold values from -0.375 to 0.375
- input_map: float32 [128, 256], replicated, may hold values from -0.5 to 0.5
Outputs:
- states: float32 [4096, 256], P(('row', 'col'))
- adjoint: float32 [4096, 256], P(('row', 'col'))
- weight_grad: float32 [256, 256], replicated
- input_grad: float32 [128, 256], replicated
Inputs may be any that keep to these rules, and one draw needn't show every extreme that they name: `tile_rows`: together with tile_cols, the slots of one device name distinct tiles. `tile_cols`: together with tile_rows, the slots of one device name distinct tiles. `tile_live`: on each device the live slots come first; every device has at least a quarter of its 4 slots live (and at least one), and some device has all 4 live. `tile_values`: roughly half of the entries of each tile are nonzero; nonzero weights lie in (0, 1].
All inputs are finite; a program needn't handle non-finite values.
Results may differ from a plain program's by a relative error of at most 0.012.
Values may be sent and summed in bfloat16 or wider, within the bound.
A program may use at most 64 MiB of HBM per device.

v0:
```python
import math

import jax
import jax.numpy as jnp
from jax import lax
from jax.sharding import PartitionSpec as P

PRECISION_HIGH = lax.Precision.HIGHEST


def spread_forward(values, rows_here, cols_here, live_here, gathered, first_tile, out_count):
    blocks = gathered.reshape(-1, values.shape[1], gathered.shape[1])
    picked = jnp.take(blocks, rows_here, axis=0)
    matrix_products = jnp.einsum("tab,taf->tbf", values, picked, preferred_element_type=jnp.float32)
    offset = cols_here - first_tile
    inside = (live_here == 1) & (offset >= 0) & (offset < out_count)
    labels = jnp.where(inside, offset, out_count)
    return jax.ops.segment_sum(matrix_products, labels, num_segments=out_count)


def spread_adjoint(values, rows_here, cols_here, live_here, gathered, first_tile, out_count):
    blocks = gathered.reshape(-1, values.shape[1], gathered.shape[1])
    picked = jnp.take(blocks, cols_here, axis=0)
    matrix_products = jnp.einsum("tab,tbf->taf", values, picked, preferred_element_type=jnp.float32)
    offset = rows_here - first_tile
    inside = (live_here == 1) & (offset >= 0) & (offset < out_count)
    labels = jnp.where(inside, offset, out_count)
    return jax.ops.segment_sum(matrix_products, labels, num_segments=out_count)


def on_device(
    starting_state,
    features,
    cotangent,
    degrees,
    tile_values,
    tile_rows,
    tile_cols,
    tile_live,
    weight,
    input_map,
):
    values = tile_values[0, 0]
    rows_here = tile_rows[0, 0]
    cols_here = tile_cols[0, 0]
    live_here = tile_live[0, 0]
    node_count = starting_state.shape[0]
    width = starting_state.shape[1]
    block = values.shape[1]
    row_devices = lax.axis_size("row")
    col_devices = lax.axis_size("col")
    tile_row_count = col_devices * node_count // block
    tile_col_count = row_devices * node_count // block
    reciprocal_square_root = lax.rsqrt(degrees.astype(jnp.float32))[:, None]
    driving = jnp.dot(features, input_map, precision=PRECISION_HIGH)
    states = starting_state
    scaled = (reciprocal_square_root * states).astype(jnp.bfloat16)
    gathered = lax.all_gather(scaled, "col", axis=0, tiled=True)
    partial_result_value = spread_forward(
        values, rows_here, cols_here, live_here, gathered, 0, tile_col_count
    )
    partial_result_value = partial_result_value.reshape(row_devices * node_count, width).astype(
        jnp.bfloat16
    )
    own_rows = lax.psum_scatter(
        partial_result_value, "row", scatter_dimension=0, tiled=True
    ).astype(jnp.float32)
    summed = reciprocal_square_root * own_rows
    states = jnp.tanh(jnp.dot(summed, weight, precision=PRECISION_HIGH) + driving)
    slopes = 1.0 - states * states
    adjoint = cotangent
    scaled = (reciprocal_square_root * (slopes * adjoint)).astype(jnp.bfloat16)
    gathered = lax.all_gather(scaled, "row", axis=0, tiled=True)
    partial_result_value = spread_adjoint(
        values, rows_here, cols_here, live_here, gathered, 0, tile_row_count
    )
    partial_result_value = partial_result_value.reshape(col_devices * node_count, width).astype(
        jnp.bfloat16
    )
    pulled = reciprocal_square_root * lax.psum_scatter(
        partial_result_value, "col", scatter_dimension=0, tiled=True
    ).astype(jnp.float32)
    adjoint = cotangent + jnp.dot(pulled, weight.T, precision=PRECISION_HIGH)
    masked = slopes * adjoint
    factor = 1.0 / math.sqrt(node_count * row_devices * col_devices)
    weight_part = jnp.dot(summed.T, masked, precision=PRECISION_HIGH)
    input_part = jnp.dot(features.T, masked, precision=PRECISION_HIGH)
    weight_grad, input_grad = lax.psum((weight_part, input_part), ("row", "col"))
    return (states, adjoint, weight_grad * factor, input_grad * factor)


def solution(mesh):
    return jax.shard_map(
        on_device,
        mesh=mesh,
        in_specs=(
            P(("row", "col"), None),
            P(("row", "col"), None),
            P(("row", "col"), None),
            P(("row", "col")),
            P("row", "col", None, None, None),
            P("row", "col", None),
            P("row", "col", None),
            P("row", "col", None),
            P(),
            P(),
        ),
        out_specs=(P(("row", "col"), None), P(("row", "col"), None), P(), P()),
        check_vma=False,
    )
```

profile of v0, /device:TPU:0, one launch (start us, length us, event | category | flops | bytes accessed | tf_op | source)
XLA Modules:
  0.0 240.8 jit_solution(16677926835895000539)
XLA Ops:
  7.2 0.7 convert_rsqrt_fusion
  7.9 1.0 multiply_convert_fusion.1
  8.9 10.5 %all_gather.6 = bf16[512,256]{1,0:T(8,128)(2,1)S(1)} all-gather(bf16[128,256]{1,0:T(8,128)(2,1)S(1)} %multiply_convert_fusion.1), channel_id=1, replica_groups=mesh['row'=8,'col'=4] {'col'}, dimensions={0}, use_global_device_ids=true | all-gather | bytes 327680 | tf_op jit(solution)/shard_map/all_gather | solution.py:58
  19.4 0.6 copy-done.9
  20.1 0.6 gather_fusion
  20.7 0.3 copy-done.3
  21.0 0.3 convolution_bitcast_fusion.1
  21.6 0.9 scatter_fusion
  22.5 0.8 convert_element_type.29
  23.5 0.7 copy-done.5
  24.6 30.4 %reduce-scatter.3.cloned.1.call-done = bf16[128,256]{1,0:T(8,128)(2,1)} async-done(((bf16[1024,256]{1,0:T(8,128)(2,1)}), bf16[128,256]{1,0:T(8,128)(2,1)}) %reduce-scatter.3.cloned.1.call-update) | async-done | bytes 65552 | tf_op jit(solution)/shard_map/reduce_scatter | solution.py:65
  55.0 1.2 multiply_convert_fusion
  56.2 14.9 %all_gather.7 = bf16[1024,256]{1,0:T(8,128)(2,1)S(1)} all-gather(bf16[128,256]{1,0:T(8,128)(2,1)S(1)} %get-tuple-element.18), channel_id=1, replica_groups=mesh['row'=8,'col'=4] {'row'}, dimensions={0}, use_global_device_ids=true | all-gather | bytes 589824 | tf_op jit(solution)/shard_map/all_gather | solution.py:73
  71.2 0.6 gather_fusion.1
  71.8 0.3 convolution_bitcast_fusion
  72.4 0.9 scatter_fusion.1
  73.2 0.7 convert_element_type.33
  74.0 22.7 %reduce-scatter.5.cloned.1.call-done = bf16[128,256]{1,0:T(8,128)(2,1)} async-done(((bf16[512,256]{1,0:T(8,128)(2,1)}), bf16[128,256]{1,0:T(8,128)(2,1)}) %reduce-scatter.5.cloned.1.call-update) | async-done | bytes 65552 | tf_op jit(solution)/shard_map/reduce_scatter | solution.py:80
  96.7 1.2 convolution_add_fusion
  98.0 1.0 convolution_bitcast_fusion.2
  99.1 1.2 fusion.9
  100.3 131.5 %all-reduce.3.cloned.1.call-done = (f32[256,256]{1,0:T(8,128)}, f32[128,256]{0,1:T(8,128)}) async-done(((f32[256,256]{1,0:T(8,128)}, f32[128,256]{0,1:T(8,128)}), (f32[256,256]{1,0:T(8,128)}, f32[128,256]{0,1:T(8,128)})) %all-reduce.3.cloned.1.call-update) | async-done | bytes 393232 | tf_op jit(solution)/shard_map/psum | solution.py:88
  231.8 1.7 broadcast_multiply_fusion
  233.5 0.8 copy.21
  (38 shorter events, 1.2 us)
Async XLA Ops:
  7.2 47.9 %copy-start = (f32[256,256]{1,0:T(8,128)S(1)}, f32[256,256]{1,0:T(8,128)}, u32[]{:S(2)}) copy-start(f32[256,256]{1,0:T(8,128)} %param.18) | copy-start | bytes 786436
  7.2 47.9 %reduce-scatter.3.cloned.1.call-start = ((), (), s32[]{:S(2)}) async-start(), calls=%async_computation.2 | async-start | bytes 589824 | tf_op jit(solution)/shard_map/reduce_scatter | solution.py:65
  8.9 10.5 %copy-start.10 = (s32[1,1,4]{2,1,0:T(1,128)S(1)}, s32[1,1,4]{2,1,0:T(1,128)}, u32[]{:S(2)}) copy-start(s32[1,1,4]{2,1,0:T(1,128)} %param.15) | copy-start | bytes 52
  19.4 0.7 copy-start.9
  19.4 0.7 copy-start.11
  20.1 0.9 copy-start.3
  23.4 0.8 copy-start.5
  23.4 0.9 copy-start.7
  23.4 73.3 %reduce-scatter.5.cloned.1.call-start = ((), (), s32[]{:S(2)}) async-start(), calls=%async_computation.3 | async-start | bytes 327680 | tf_op jit(solution)/shard_map/reduce_scatter | solution.py:80
  24.3 30.7 %copy-start.4 = (f32[128,256]{1,0:T(8,128)S(1)}, f32[128,256]{1,0:T(8,128)}, u32[]{:S(2)}) copy-start(f32[128,256]{1,0:T(8,128)} %param.12) | copy-start | bytes 393220
  56.2 42.8 %copy-start.1 = (f32[128,256]{1,0:T(8,128)}, f32[128,256]{1,0:T(8,128)S(1)}, u32[]{:S(2)}) copy-start(f32[128,256]{1,0:T(8,128)S(1)} %get-tuple-element.19) | copy-start | bytes 393220
  74.0 157.8 %all-reduce.3.cloned.1.call-start = ((), (), s32[]{:S(2)}) async-start(), calls=%async_computation.4 | async-start | bytes 786432 | tf_op jit(solution)/shard_map/psum | solution.py:88
  98.0 1.1 copy-start.2
  98.0 1.1 copy-start.6
  231.8 1.7 copy-start.8
Sparse Core Ops, SparseCore 0:
  23.5 31.4 reduce-scatter.2
  74.1 22.5 reduce-scatter.4
  102.7 129.0 all-reduce.2
where the time goes:
time: 241 us
  waiting for transfers between devices  185 us (77%)
  blocking collectives  25.4 us (11%)
  between operations  14 us (6%)
  other arithmetic  6.78 us (3%)
  matrix products  5.59 us (2%)
  local copies, waits for them, and re-layouts  4.24 us (2%)
    psum x1, waiting for transfers between devices, on_device(): lax.psum((weight_part, input_part), ('row', 'col'))  132 us
    reduce_scatter x1, waiting for transfers between devices, on_device(): lax.psum_scatter(partial_result_value, 'row', scatter_dimension=0, tiled=...  30.4 us
    reduce_scatter x1, waiting for transfers between devices, on_device(): lax.psum_scatter(partial_result_value, 'col', scatter_dimension=0, tiled=...  22.7 us
    all_gather x1, blocking collectives, on_device(): gathered = lax.all_gather(scaled, 'row', axis=0, tiled=True)  14.9 us
    all_gather x1, blocking collectives, on_device(): gathered = lax.all_gather(scaled, 'col', axis=0, tiled=True)  10.5 us
  transfers between devices with their start and end apart: 3, of which 3 were waited for; matrix products, arithmetic and copies ran while one was open for 0% of the time, Pallas kernels for 0%

commit v1 on v0

v1 whole, which is shorter than its diff:
```python
import functools
import math

import jax
import jax.numpy as jnp
from jax import lax
from jax.experimental import pallas as pl
from jax.experimental.pallas import tpu as pltpu
from jax.sharding import PartitionSpec as P

PRECISION_HIGH = lax.Precision.HIGHEST
MESH = pl.DeviceIdType.MESH
VMEM_PLAN = 40 * 2**20
F32 = jnp.float32
BF16 = jnp.bfloat16


def spread(values, picked_at, label_at, live_here, gathered, out_count, equation):
    blocks = gathered.reshape(-1, values.shape[1], gathered.shape[1])
    picked = jnp.take(blocks, picked_at, axis=0)
    products = jnp.einsum(equation, values, picked, preferred_element_type=F32)
    labels = jnp.where(live_here == 1, label_at, out_count)
    return jax.ops.segment_sum(products, labels, num_segments=out_count)


def collective_path(
    starting_state, features, cotangent, degrees, tile_values,
    tile_rows, tile_cols, tile_live, weight, input_map,
):
    values, rows_here = tile_values[0, 0], tile_rows[0, 0]
    cols_here, live_here = tile_cols[0, 0], tile_live[0, 0]
    nodes, width = starting_state.shape
    block = values.shape[1]
    n_row, n_col = lax.axis_size("row"), lax.axis_size("col")
    inverse_root = lax.rsqrt(degrees.astype(F32))[:, None]
    driving = jnp.dot(features, input_map, precision=PRECISION_HIGH)
    scaled = (inverse_root * starting_state).astype(BF16)
    gathered = lax.all_gather(scaled, "col", axis=0, tiled=True)
    partial = spread(
        values, rows_here, cols_here, live_here, gathered, n_row * nodes // block, "tab,taf->tbf"
    )
    partial = partial.reshape(n_row * nodes, width).astype(BF16)
    own = lax.psum_scatter(partial, "row", scatter_dimension=0, tiled=True).astype(F32)
    summed = inverse_root * own
    states = jnp.tanh(jnp.dot(summed, weight, precision=PRECISION_HIGH) + driving)
    slopes = 1.0 - states * states
    scaled = (inverse_root * (slopes * cotangent)).astype(BF16)
    gathered = lax.all_gather(scaled, "row", axis=0, tiled=True)
    partial = spread(
        values, cols_here, rows_here, live_here, gathered, n_col * nodes // block, "tab,tbf->taf"
    )
    partial = partial.reshape(n_col * nodes, width).astype(BF16)
    own = lax.psum_scatter(partial, "col", scatter_dimension=0, tiled=True).astype(F32)
    pulled = inverse_root * own
    adjoint = cotangent + jnp.dot(pulled, weight.T, precision=PRECISION_HIGH)
    masked = slopes * adjoint
    factor = 1.0 / math.sqrt(nodes * n_row * n_col)
    weight_part = jnp.dot(summed.T, masked, precision=PRECISION_HIGH)
    input_part = jnp.dot(features.T, masked, precision=PRECISION_HIGH)
    weight_grad, input_grad = lax.psum((weight_part, input_part), ("row", "col"))
    return states, adjoint, weight_grad * factor, input_grad * factor


def kernel(
    n_row, n_col, factor,
    state_ref, feat_ref, cot_ref, deg_ref, val_ref, rows_ref, cols_ref, live_ref, w_ref, map_ref,
    states_ref, adjoint_ref, grad_ref,
    fwd_l, adj_l, gath, core_send, core_recv, z_send, z_recv, gath2, q_send, q_recv,
    g_send, g_recv, s_all,
    a_s, a_r, b_s, b_r, c_s, c_r, d_s, d_r, e_s, e_r, f_s, f_r, g_s, g_r, h_s, h_r, i_s, i_r,
):
    r, c = lax.axis_index("row"), lax.axis_index("col")
    n_z = n_row // 2
    plane = 2 * n_col
    z, core = r // 2, r % 2
    other = 1 - core
    nodes, width = state_ref.shape
    slots, block = val_ref.shape[2], val_ref.shape[3]
    place = c * 2 + core

    def z_peer(d):
        return (2 * ((z + d) % n_z) + core, c)

    def plane_peer(e):
        p = (place + e) % plane
        return p, (2 * z + p % 2, p // 2)

    def send(src, dst, s_sem, r_sem, device):
        copy = pltpu.make_async_remote_copy(
            src_ref=src, dst_ref=dst, send_sem=s_sem, recv_sem=r_sem,
            device_id=device, device_id_type=MESH,
        )
        copy.start()
        return copy

    started = []

    barrier = pltpu.get_barrier_semaphore()
    for d in range(1, n_z):
        pl.semaphore_signal(barrier, inc=1, device_id=z_peer(d), device_id_type=MESH)
    for e in range(1, plane):
        pl.semaphore_signal(barrier, inc=1, device_id=plane_peer(e)[1], device_id_type=MESH)

    wide = jnp.broadcast_to(deg_ref[...].astype(F32), (nodes, nodes))
    inv = lax.rsqrt(wide.T)
    inv = jnp.concatenate([inv] * (width // nodes), axis=1)
    gath[c] = (inv * state_ref[...]).astype(BF16)

    pl.semaphore_wait(barrier, n_z - 1 + plane - 1)

    a_copies = []
    for d in range(1, n_col):
        a_copies.append(
            send(gath.at[c], gath.at[c], a_s.at[d - 1], a_r.at[d - 1], (r, (c + d) % n_col))
        )

    for t in range(slots):
        tile = val_ref[0, 0, t].astype(F32)
        turned = tile.T
        at = pl.ds(t * block, block)
        live = live_ref[0, 0, t] == 1
        for k in range(2):
            for d in range(n_z):
                goal = 2 * ((z + d) % n_z) + (other if k == 0 else core)
                keep = jnp.where(live & (cols_ref[0, 0, t] == goal), 1.0, 0.0).astype(F32)
                fwd_l[k, d, :, at] = (turned * keep).astype(BF16)
        for d in range(n_col):
            keep = jnp.where(live & (rows_ref[0, 0, t] == (c + d) % n_col), 1.0, 0.0).astype(F32)
            adj_l[d, :, at] = (tile * keep).astype(BF16)
    feat = feat_ref[...]
    driving = jnp.dot(feat.astype(BF16), map_ref[...].astype(BF16), preferred_element_type=F32)

    for copy in a_copies:
        copy.wait_recv()
    started += a_copies

    picked = jnp.concatenate([gath[rows_ref[0, 0, t]] for t in range(slots)], axis=0)
    order = list(range(1, n_z)) + [0]
    b_copies = {}
    for d in order:
        core_send[d] = jnp.dot(fwd_l[0, d], picked, preferred_element_type=F32).astype(BF16)
        b_copies[d] = send(
            core_send.at[d], core_recv.at[d], b_s.at[d], b_r.at[d], (2 * z + other, c)
        )
    c_copies = []
    for d in order:
        mine = jnp.dot(fwd_l[1, d], picked, preferred_element_type=F32)
        b_copies[d].wait_recv()
        total = mine + core_recv[d].astype(F32)
        if d:
            z_send[d - 1] = total.astype(BF16)
            c_copies.append(
                send(z_send.at[d - 1], z_recv.at[d - 1], c_s.at[d - 1], c_r.at[d - 1], z_peer(d))
            )
    for d in range(1, n_z):
        c_copies[d - 1].wait_recv()
        total = total + z_recv[d - 1].astype(F32)
    started += list(b_copies.values()) + c_copies

    summed = inv * total
    states = jnp.tanh(
        jnp.dot(summed.astype(BF16), w_ref[...].astype(BF16), preferred_element_type=F32) + driving
    )
    slopes = 1.0 - states * states
    cot = cot_ref[...]
    gath2[r] = (inv * (slopes * cot)).astype(BF16)

    d_copies = [
        send(gath2.at[r], gath2.at[r], d_s.at[d - 1], d_r.at[d - 1], z_peer(d))
        for d in range(1, n_z)
    ]
    e_copies = [send(gath2.at[r], gath2.at[r], e_s.at[0], e_r.at[0], (2 * z + other, c))]
    states_ref[...] = states
    both_t = jnp.concatenate([summed.T, feat.T], axis=0).astype(BF16)
    for d in range(1, n_z):
        d_copies[d - 1].wait_recv()
        slot = 2 * ((z + n_z - d) % n_z) + core
        e_copies.append(
            send(gath2.at[slot], gath2.at[slot], e_s.at[d], e_r.at[d], (2 * z + other, c))
        )
    for copy in e_copies:
        copy.wait_recv()
    started += d_copies + e_copies

    picked = jnp.concatenate([gath2[cols_ref[0, 0, t]] for t in range(slots)], axis=0)
    f_copies = []
    for d in range(1, n_col):
        q_send[d - 1] = jnp.dot(adj_l[d], picked, preferred_element_type=F32).astype(BF16)
        f_copies.append(
            send(q_send.at[d - 1], q_recv.at[d - 1], f_s.at[d - 1], f_r.at[d - 1], (r, (c + d) % n_col))
        )
    total = jnp.dot(adj_l[0], picked, preferred_element_type=F32)
    for d in range(1, n_col):
        f_copies[d - 1].wait_recv()
        total = total + q_recv[d - 1].astype(F32)
    started += f_copies
    pulled = inv * total
    adjoint = cot + lax.dot_general(
        pulled.astype(BF16), w_ref[...].astype(BF16), (((1,), (1,)), ((), ())),
        preferred_element_type=F32,
    )
    masked = (slopes * adjoint).astype(BF16)

    grad = jnp.dot(both_t, masked, preferred_element_type=F32)
    g_send[...] = grad.reshape(g_send.shape).astype(BF16)
    g_copies = []
    for e in range(1, plane):
        p, device = plane_peer(e)
        g_copies.append(
            send(g_send.at[p], g_recv.at[e - 1], g_s.at[e - 1], g_r.at[e - 1], device)
        )
    adjoint_ref[...] = adjoint
    total = g_send[place].astype(F32)
    for e in range(1, plane):
        g_copies[e - 1].wait_recv()
        total = total + g_recv[e - 1].astype(F32)
    s_all[z] = total.astype(BF16)
    h_copies = [
        send(s_all.at[z], s_all.at[z], h_s.at[d - 1], h_r.at[d - 1], z_peer(d))
        for d in range(1, n_z)
    ]
    for copy in h_copies:
        copy.wait_recv()
    total = s_all[0].astype(F32)
    for d in range(1, n_z):
        total = total + s_all[d].astype(F32)
    grad_ref[place] = (total * factor).astype(BF16)
    i_copies = [
        send(grad_ref.at[place], grad_ref.at[place], i_s.at[e - 1], i_r.at[e - 1], plane_peer(e)[1])
        for e in range(1, plane)
    ]
    for copy in i_copies:
        copy.wait_recv()
    started += g_copies + h_copies + i_copies
    for copy in started:
        copy.wait_send()


def fits(n_row, n_col, nodes, width, inputs, slots, block):
    plan = 4 * slots * block * block * (n_row + n_col)
    plan += 8 * nodes * width * (n_row + n_col)
    plane = 2 * n_col
    return (
        plan <= VMEM_PLAN
        and nodes == block
        and width % nodes == 0
        and n_row % 2 == 0
        and (width + inputs) % (16 * plane) == 0
    )


def kernel_path(
    starting_state, features, cotangent, degrees, tile_values,
    tile_rows, tile_cols, tile_live, weight, input_map,
):
    n_row, n_col = lax.axis_size("row"), lax.axis_size("col")
    n_z, plane = n_row // 2, 2 * n_col
    nodes, width = starting_state.shape
    inputs = features.shape[1]
    slots, block = tile_values.shape[2], tile_values.shape[3]
    factor = 1.0 / math.sqrt(nodes * n_row * n_col)
    rows_each = (width + inputs) // plane
    vmem = pl.BlockSpec(memory_space=pltpu.VMEM)
    smem = pl.BlockSpec(memory_space=pltpu.SMEM)
    piece = (nodes, width)
    sems = []
    for count in (n_col - 1, n_z, n_z - 1, n_z - 1, n_z, n_col - 1, plane - 1, n_z - 1, plane - 1):
        sems += [pltpu.SemaphoreType.DMA((count,)), pltpu.SemaphoreType.DMA((count,))]
    states, adjoint, grads = pl.pallas_call(
        functools.partial(kernel, n_row, n_col, factor),
        out_shape=(
            jax.ShapeDtypeStruct(piece, F32),
            jax.ShapeDtypeStruct(piece, F32),
            jax.ShapeDtypeStruct((plane, rows_each, width), BF16),
        ),
        in_specs=[vmem] * 5 + [smem] * 3 + [vmem] * 2,
        out_specs=(vmem, vmem, vmem),
        scratch_shapes=[
            pltpu.VMEM((2, n_z, block, slots * block), BF16),
            pltpu.VMEM((n_col, block, slots * block), BF16),
            pltpu.VMEM((n_col,) + piece, BF16),
            pltpu.VMEM((n_z,) + piece, BF16),
            pltpu.VMEM((n_z,) + piece, BF16),
            pltpu.VMEM((n_z - 1,) + piece, BF16),
            pltpu.VMEM((n_z - 1,) + piece, BF16),
            pltpu.VMEM((n_row,) + piece, BF16),
            pltpu.VMEM((n_col - 1,) + piece, BF16),
            pltpu.VMEM((n_col - 1,) + piece, BF16),
            pltpu.VMEM((plane, rows_each, width), BF16),
            pltpu.VMEM((plane - 1, rows_each, width), BF16),
            pltpu.VMEM((n_z, rows_each, width), BF16),
        ] + sems,
        compiler_params=pltpu.CompilerParams(collective_id=0, has_side_effects=True),
        name="graph_window",
    )(
        starting_state, features, cotangent, degrees.reshape(1, -1), tile_values,
        tile_rows, tile_cols, tile_live, weight, input_map,
    )
    grads = grads.reshape(width + inputs, width).astype(F32)
    return states, adjoint, grads[:width], grads[width:]


def on_device(*args):
    nodes, width = args[0].shape
    sizes = (nodes, width, args[1].shape[1], args[4].shape[2], args[4].shape[3])
    if fits(lax.axis_size("row"), lax.axis_size("col"), *sizes):
        return kernel_path(*args)
    return collective_path(*args)


def solution(mesh):
    nodes_split = P(("row", "col"), None)
    tiles_split = P("row", "col", None)
    return jax.shard_map(
        on_device,
        mesh=mesh,
        in_specs=(
            nodes_split, nodes_split, nodes_split, P(("row", "col")),
            P("row", "col", None, None, None), tiles_split, tiles_split, tiles_split, P(), P(),
        ),
        out_specs=(nodes_split, nodes_split, P(), P()),
        check_vma=False,
    )
```

time: 241 us -> 53.8 us (0.22)
  waiting for transfers between devices: 185 us -> 0 us
  Pallas kernels: 0 us -> 48.7 us
  blocking collectives: 25.4 us -> 0 us
  between operations: 14 us -> 0.65 us
  other arithmetic: 6.78 us -> 0.95 us
  matrix products: 5.59 us -> 0 us
    psum x1 -> x0, waiting for transfers between devices: 132 us -> none  [on_device(): lax.psum((weight_part, input_part), ('row', 'col'))]
    reduce_scatter x2 -> x0, waiting for transfers between devices: 53.1 us -> none  [the longest x1 30.4 us: on_device(): lax.psum_scatter(partial_result_value, 'row', scatter_dimension=0, tiled=...]
    pallas_call x0 -> x1, Pallas kernels: none -> 48.7 us  [kernel_path(): pl.pallas_call(functools.partial(kernel, n_row, n_col, factor), out_shape...]
    all_gather x2 -> x0, blocking collectives: 25.4 us -> none  [the longest x1 14.9 us: on_device(): gathered = lax.all_gather(scaled, 'row', axis=0, tiled=True)]
    dot_general x7 -> x0, matrix products: 5.59 us -> none  [the longest x1 1.24 us: on_device(): adjoint = cotangent + jnp.dot(pulled, weight.T, precision=PRECISION_HIGH)]
  transfers between devices with their start and end apart: 3 -> 0, of which waited for: 3 -> 0; matrix products, arithmetic and copies ran while one was open for 0% -> 0% of each run, Pallas kernels for 0% -> 0%
where the time goes in v1:
time: 53.8 us; the launch traced here: 53.6 us
  Pallas kernels  48.7 us (91%)
  local copies, waits for them, and re-layouts  3.24 us (6%)
  other arithmetic  0.95 us (2%)
  between operations  0.65 us (1%)
    pallas_call x1, Pallas kernels, kernel_path(): pl.pallas_call(functools.partial(kernel, n_row, n_col, factor), out_shape...  48.7 us
    unnamed x6, local copies, waits for them, and re-layouts  1.86 us
    slice x2, local copies, waits for them, and re-layouts, kernel_path(): return (states, adjoint, grads[:width], grads[width:])  1.38 us

profile of v1, /device:TPU:0, one launch (start us, length us, event | category | flops | bytes accessed | tf_op | source)
XLA Modules:
  0.0 53.6 jit_solution(4446779019414793623)
XLA Ops:
  0.6 48.7 %graph_window.1 = (f32[128,256]{1,0:T(8,128)}, f32[128,256]{1,0:T(8,128)}, bf16[8,48,256]{2,1,0:T(8,128)(2,1)}) custom-call(f32[128,256]{1,0:T(8,128)} %state_ref.1, f32[128,128]{1,0:T(8,128)} %feat_ref.1, f32[128,256]{1,0:T(8,128)} %cot_ref.1, s32[1,128]{1,0:T(1,128)} %bitcast.4, bf16[1,1,4,128,128]{4,3,2,1,0:T(8,128)(2,1)} %val_ref.1, ...), custom_call_target="tpu_custom_call" | custom-call | tf_op jit(solution)/shard_map/graph_window/pallas_call | solution.py:269
  49.4 1.0 %bitcast_convert_fusion = f32[384,256]{1,0:T(8,128)S(1)} fusion(bf16[8,48,256]{2,1,0:T(8,128)(2,1)} %get-tuple-element.9), kind=kLoop, calls=%fused_computation | loop fusion | flops 98304 | bytes 589824 | tf_op jit(solution)/shard_map/convert_element_type | solution.py:299
  50.3 0.7 %slice.9 = f32[128,256]{1,0:T(8,128)} slice(f32[384,256]{1,0:T(8,128)S(1)} %bitcast_convert_fusion), slice={[256:384], [0:256]} | slice | bytes 262144 | tf_op jit(solution)/shard_map/slice | solution.py:300
  51.0 0.0 copy-start.1
  51.0 0.7 %slice.8 = f32[256,256]{1,0:T(8,128)} slice(f32[384,256]{1,0:T(8,128)S(1)} %bitcast_convert_fusion), slice={[0:256], [0:256]} | slice | bytes 524288 | tf_op jit(solution)/shard_map/slice | solution.py:300
  51.7 0.3 copy-done.1
  52.0 0.0 copy-start
  52.0 0.7 %copy.16 = f32[128,256]{1,0:T(8,128)} copy(f32[128,256]{1,0:T(8,128)S(1)} %copy-done.1) | data formatting | bytes 262144
  52.6 0.3 copy-done
  52.9 0.7 %copy.17 = f32[128,256]{1,0:T(8,128)} copy(f32[128,256]{1,0:T(8,128)S(1)} %copy-done) | data formatting | bytes 262144
Async XLA Ops:
  51.0 1.0 %copy-start.1 = (f32[128,256]{1,0:T(8,128)S(1)}, f32[128,256]{1,0:T(8,128)}, u32[]{:S(2)}) copy-start(f32[128,256]{1,0:T(8,128)} %get-tuple-element.14) | copy-start | bytes 393220
  52.0 1.0 %copy-start = (f32[128,256]{1,0:T(8,128)S(1)}, f32[128,256]{1,0:T(8,128)}, u32[]{:S(2)}) copy-start(f32[128,256]{1,0:T(8,128)} %get-tuple-element.15) | copy-start | bytes 393220

commit v2 on v1

--- a/solution.py
+++ b/solution.py
@@ -10,7 +10,9 @@
 
 PRECISION_HIGH = lax.Precision.HIGHEST
 MESH = pl.DeviceIdType.MESH
-VMEM_PLAN = 40 * 2**20
+VMEM_PLAN = 12 * 2**20
+KERNEL_LIMIT = 24 * 2**20
+FINISH_LIMIT = 8 * 2**20
 F32 = jnp.float32
 BF16 = jnp.bfloat16
 
@@ -63,8 +65,9 @@
 
 def kernel(
     n_row, n_col, factor,
-    state_ref, feat_ref, cot_ref, deg_ref, val_ref, rows_ref, cols_ref, live_ref, w_ref, map_ref,
+    state_in, feat_in, cot_in, deg_in, val_in, rows_in, cols_in, live_in, w_in, map_in,
     states_ref, adjoint_ref, grad_ref,
+    state_ref, feat_ref, cot_ref, deg_ref, val_ref, rows_ref, cols_ref, live_ref, w_ref, map_ref, in_sem,
     fwd_l, adj_l, gath, core_send, core_recv, z_send, z_recv, gath2, q_send, q_recv,
     g_send, g_recv, s_all,
     a_s, a_r, b_s, b_r, c_s, c_r, d_s, d_r, e_s, e_r, f_s, f_r, g_s, g_r, h_s, h_r, i_s, i_r,
@@ -101,6 +104,19 @@
     for e in range(1, plane):
         pl.semaphore_signal(barrier, inc=1, device_id=plane_peer(e)[1], device_id_type=MESH)
 
+    pairs = (
+        (deg_in, deg_ref), (state_in, state_ref), (rows_in, rows_ref), (cols_in, cols_ref),
+        (live_in, live_ref), (val_in, val_ref), (feat_in, feat_ref), (map_in, map_ref),
+        (w_in, w_ref), (cot_in, cot_ref),
+    )
+    loads = [
+        pltpu.make_async_copy(src, dst, in_sem.at[i]) for i, (src, dst) in enumerate(pairs)
+    ]
+    for load in loads:
+        load.start()
+    for load in loads[:2]:
+        load.wait()
+
     wide = jnp.broadcast_to(deg_ref[...].astype(F32), (nodes, nodes))
     inv = lax.rsqrt(wide.T)
     inv = jnp.concatenate([inv] * (width // nodes), axis=1)
@@ -113,6 +129,9 @@
         a_copies.append(
             send(gath.at[c], gath.at[c], a_s.at[d - 1], a_r.at[d - 1], (r, (c + d) % n_col))
         )
+
+    for load in loads[2:]:
+        load.wait()
 
     for t in range(slots):
         tile = val_ref[0, 0, t].astype(F32)
@@ -236,6 +255,14 @@
         copy.wait_send()
 
 
+def finish(states_in, adjoint_in, grads_in, states_out, adjoint_out, weight_out, input_out):
+    states_out[...] = states_in[...]
+    adjoint_out[...] = adjoint_in[...]
+    grads = grads_in[...].astype(F32).reshape(-1, grads_in.shape[2])
+    weight_out[...] = grads[: weight_out.shape[0]]
+    input_out[...] = grads[weight_out.shape[0] :]
+
+
 def fits(n_row, n_col, nodes, width, inputs, slots, block):
     plan = 4 * slots * block * block * (n_row + n_col)
     plan += 8 * nodes * width * (n_row + n_col)
@@ -261,7 +288,15 @@
     factor = 1.0 / math.sqrt(nodes * n_row * n_col)
     rows_each = (width + inputs) // plane
     vmem = pl.BlockSpec(memory_space=pltpu.VMEM)
-    smem = pl.BlockSpec(memory_space=pltpu.SMEM)
+    hbm = pl.BlockSpec(memory_space=pltpu.HBM)
+    operands = (
+        starting_state, features, cotangent, degrees.reshape(1, -1), tile_values,
+        tile_rows, tile_cols, tile_live, weight, input_map,
+    )
+    held = [
+        (pltpu.SMEM if 5 <= i < 8 else pltpu.VMEM)(x.shape, x.dtype)
+        for i, x in enumerate(operands)
+    ]
     piece = (nodes, width)
     sems = []
     for count in (n_col - 1, n_z, n_z - 1, n_z - 1, n_z, n_col - 1, plane - 1, n_z - 1, plane - 1):
@@ -273,9 +308,10 @@
             jax.ShapeDtypeStruct(piece, F32),
             jax.ShapeDtypeStruct((plane, rows_each, width), BF16),
         ),
-        in_specs=[vmem] * 5 + [smem] * 3 + [vmem] * 2,
+        in_specs=[hbm] * len(operands),
         out_specs=(vmem, vmem, vmem),
-        scratch_shapes=[
+        scratch_shapes=held + [
+            pltpu.SemaphoreType.DMA((len(operands),)),
             pltpu.VMEM((2, n_z, block, slots * block), BF16),
             pltpu.VMEM((n_col, block, slots * block), BF16),
             pltpu.VMEM((n_col,) + piece, BF16),
@@ -290,14 +326,24 @@
             pltpu.VMEM((plane - 1, rows_each, width), BF16),
             pltpu.VMEM((n_z, rows_each, width), BF16),
         ] + sems,
-        compiler_params=pltpu.CompilerParams(collective_id=0, has_side_effects=True),
+        compiler_params=pltpu.CompilerParams(
+            collective_id=0, has_side_effects=True, vmem_limit_bytes=KERNEL_LIMIT
+        ),
         name="graph_window",
-    )(
-        starting_state, features, cotangent, degrees.reshape(1, -1), tile_values,
-        tile_rows, tile_cols, tile_live, weight, input_map,
-    )
-    grads = grads.reshape(width + inputs, width).astype(F32)
-    return states, adjoint, grads[:width], grads[width:]
+    )(*[pltpu.with_memory_space_constraint(x, pltpu.HBM) for x in operands])
+    return pl.pallas_call(
+        finish,
+        out_shape=(
+            jax.ShapeDtypeStruct(piece, F32),
+            jax.ShapeDtypeStruct(piece, F32),
+            jax.ShapeDtypeStruct((width, width), F32),
+            jax.ShapeDtypeStruct((inputs, width), F32),
+        ),
+        in_specs=[vmem] * 3,
+        out_specs=(vmem,) * 4,
+        compiler_params=pltpu.CompilerParams(vmem_limit_bytes=FINISH_LIMIT),
+        name="finish",
+    )(states, adjoint, grads)
 
 
 def on_device(*args):

time: 53.8 us -> 48.5 us (0.901)
  local copies, waits for them, and re-layouts: 3.24 us -> 0 us
  Pallas kernels: 48.7 us -> 47.7 us
  other arithmetic: 0.95 us -> 0 us
    pallas_call x1, Pallas kernels: 48.7 us -> 46.8 us  [kernel_path(): pl.pallas_call(functools.partial(kernel, n_row, n_col, factor), out_shape...]
    unnamed x6 -> x0, local copies, waits for them, and re-layouts: 1.86 us -> none
    slice x2 -> x0, local copies, waits for them, and re-layouts: 1.38 us -> none  [kernel_path(): return (states, adjoint, grads[:width], grads[width:])]
    convert_element_type x1 -> x0, other arithmetic: 0.95 us -> none  [kernel_path(): grads = grads.reshape(width + inputs, width).astype(F32)]
    pallas_call x0 -> x1, Pallas kernels: none -> 0.86 us  [kernel_path(): pl.pallas_call(finish, out_shape=(jax.ShapeDtypeStruct(piece, F32), jax.S...]
where the time goes in v2:
time: 48.5 us; the launch traced here: 48.3 us
  Pallas kernels  47.7 us (98%)
  between operations  0.64 us (1%)
    pallas_call x1, Pallas kernels, kernel_path(): pl.pallas_call(functools.partial(kernel, n_row, n_col, factor), out_shape...  46.8 us

profile of v2, /device:TPU:0, one launch (start us, length us, event | category | flops | bytes accessed | tf_op | source)
XLA Modules:
  0.0 48.3 jit_solution(4914009360765379696)
XLA Ops:
  0.6 46.8 %graph_window.1 = (f32[128,256]{1,0:T(8,128)S(1)}, f32[128,256]{1,0:T(8,128)S(1)}, bf16[8,48,256]{2,1,0:T(8,128)(2,1)S(1)}) custom-call(f32[128,256]{1,0:T(8,128)} %state_in.1, f32[128,128]{1,0:T(8,128)} %feat_in.1, f32[128,256]{1,0:T(8,128)} %cot_in.1, s32[1,128]{1,0:T(1,128)} %bitcast.1, bf16[1,1,4,128,128]{4,3,2,1,0:T(8,128)(2,1)} %val_in.1, ...), custom_call_target="tpu_custom_call" | custom-call | tf_op jit(solution)/shard_map/graph_window/pallas_call | solution.py:304
  47.5 0.9 %finish.1 = (f32[128,256]{1,0:T(8,128)}, f32[128,256]{1,0:T(8,128)}, f32[256,256]{1,0:T(8,128)}, f32[128,256]{1,0:T(8,128)}) custom-call(f32[128,256]{1,0:T(8,128)S(1)} %get-tuple-element.7.states_in, f32[128,256]{1,0:T(8,128)S(1)} %get-tuple-element.8.adjoint_in, bf16[8,48,256]{2,1,0:T(8,128)(2,1)S(1)} %get-tuple-element.9.grads_in), custom_call_target="tpu_custom_call" | custom-call | tf_op jit(solution)/shard_map/finish/pallas_call | solution.py:334

commit v3 on v2

--- a/solution.py
+++ b/solution.py
@@ -15,6 +15,7 @@
 FINISH_LIMIT = 8 * 2**20
 F32 = jnp.float32
 BF16 = jnp.bfloat16
+LANES, SUBLANES = 128, 8
 
 
 def spread(values, picked_at, label_at, live_here, gathered, out_count, equation):
@@ -69,24 +70,20 @@
     states_ref, adjoint_ref, grad_ref,
     state_ref, feat_ref, cot_ref, deg_ref, val_ref, rows_ref, cols_ref, live_ref, w_ref, map_ref, in_sem,
     fwd_l, adj_l, gath, core_send, core_recv, z_send, z_recv, gath2, q_send, q_recv,
-    g_send, g_recv, s_all,
-    a_s, a_r, b_s, b_r, c_s, c_r, d_s, d_r, e_s, e_r, f_s, f_r, g_s, g_r, h_s, h_r, i_s, i_r,
+    g_send, g_recv,
+    a_s, a_r, b_s, b_r, c_s, c_r, d_s, d_r, e_s, e_r, f_s, f_r, g_s, g_r, h_s, h_r,
 ):
     r, c = lax.axis_index("row"), lax.axis_index("col")
     n_z = n_row // 2
-    plane = 2 * n_col
     z, core = r // 2, r % 2
     other = 1 - core
     nodes, width = state_ref.shape
     slots, block = val_ref.shape[2], val_ref.shape[3]
-    place = c * 2 + core
+    n_all = n_row * n_col
+    me = r * n_col + c
 
     def z_peer(d):
         return (2 * ((z + d) % n_z) + core, c)
-
-    def plane_peer(e):
-        p = (place + e) % plane
-        return p, (2 * z + p % 2, p // 2)
 
     def send(src, dst, s_sem, r_sem, device):
         copy = pltpu.make_async_remote_copy(
@@ -99,10 +96,11 @@
     started = []
 
     barrier = pltpu.get_barrier_semaphore()
-    for d in range(1, n_z):
-        pl.semaphore_signal(barrier, inc=1, device_id=z_peer(d), device_id_type=MESH)
-    for e in range(1, plane):
-        pl.semaphore_signal(barrier, inc=1, device_id=plane_peer(e)[1], device_id_type=MESH)
+    for k in range(1, n_all):
+        goal = (me + k) % n_all
+        pl.semaphore_signal(
+            barrier, inc=1, device_id=(goal // n_col, goal % n_col), device_id_type=MESH
+        )
 
     pairs = (
         (deg_in, deg_ref), (state_in, state_ref), (rows_in, rows_ref), (cols_in, cols_ref),
@@ -122,7 +120,7 @@
     inv = jnp.concatenate([inv] * (width // nodes), axis=1)
     gath[c] = (inv * state_ref[...]).astype(BF16)
 
-    pl.semaphore_wait(barrier, n_z - 1 + plane - 1)
+    pl.semaphore_wait(barrier, n_all - 1)
 
     a_copies = []
     for d in range(1, n_col):
@@ -154,27 +152,27 @@
     started += a_copies
 
     picked = jnp.concatenate([gath[rows_ref[0, 0, t]] for t in range(slots)], axis=0)
-    order = list(range(1, n_z)) + [0]
+    order = sorted(range(1, n_z), key=lambda d: -min(d, n_z - d)) + [0]
     b_copies = {}
     for d in order:
         core_send[d] = jnp.dot(fwd_l[0, d], picked, preferred_element_type=F32).astype(BF16)
         b_copies[d] = send(
             core_send.at[d], core_recv.at[d], b_s.at[d], b_r.at[d], (2 * z + other, c)
         )
-    c_copies = []
+    c_copies = {}
     for d in order:
         mine = jnp.dot(fwd_l[1, d], picked, preferred_element_type=F32)
         b_copies[d].wait_recv()
         total = mine + core_recv[d].astype(F32)
         if d:
             z_send[d - 1] = total.astype(BF16)
-            c_copies.append(
-                send(z_send.at[d - 1], z_recv.at[d - 1], c_s.at[d - 1], c_r.at[d - 1], z_peer(d))
+            c_copies[d] = send(
+                z_send.at[d - 1], z_recv.at[d - 1], c_s.at[d - 1], c_r.at[d - 1], z_peer(d)
             )
-    for d in range(1, n_z):
-        c_copies[d - 1].wait_recv()
+    for d in reversed(order[:-1]):
+        c_copies[d].wait_recv()
         total = total + z_recv[d - 1].astype(F32)
-    started += list(b_copies.values()) + c_copies
+    started += list(b_copies.values()) + list(c_copies.values())
 
     summed = inv * total
     states = jnp.tanh(
@@ -184,22 +182,22 @@
     cot = cot_ref[...]
     gath2[r] = (inv * (slopes * cot)).astype(BF16)
 
-    d_copies = [
-        send(gath2.at[r], gath2.at[r], d_s.at[d - 1], d_r.at[d - 1], z_peer(d))
-        for d in range(1, n_z)
-    ]
+    d_copies = {
+        d: send(gath2.at[r], gath2.at[r], d_s.at[d - 1], d_r.at[d - 1], z_peer(d))
+        for d in order[:-1]
+    }
     e_copies = [send(gath2.at[r], gath2.at[r], e_s.at[0], e_r.at[0], (2 * z + other, c))]
     states_ref[...] = states
     both_t = jnp.concatenate([summed.T, feat.T], axis=0).astype(BF16)
-    for d in range(1, n_z):
-        d_copies[d - 1].wait_recv()
+    for d in reversed(order[:-1]):
+        d_copies[d].wait_recv()
         slot = 2 * ((z + n_z - d) % n_z) + core
         e_copies.append(
             send(gath2.at[slot], gath2.at[slot], e_s.at[d], e_r.at[d], (2 * z + other, c))
         )
     for copy in e_copies:
         copy.wait_recv()
-    started += d_copies + e_copies
+    started += list(d_copies.values()) + e_copies
 
     picked = jnp.concatenate([gath2[cols_ref[0, 0, t]] for t in range(slots)], axis=0)
     f_copies = []
@@ -221,36 +219,43 @@
     masked = (slopes * adjoint).astype(BF16)
 
     grad = jnp.dot(both_t, masked, preferred_element_type=F32)
-    g_send[...] = grad.reshape(g_send.shape).astype(BF16)
-    g_copies = []
-    for e in range(1, plane):
-        p, device = plane_peer(e)
-        g_copies.append(
-            send(g_send.at[p], g_recv.at[e - 1], g_s.at[e - 1], g_r.at[e - 1], device)
-        )
+    halves = width // LANES
+    groups = n_all // halves
+    for h in range(halves):
+        part = grad[:, h * LANES : (h + 1) * LANES]
+        g_send[h * groups : (h + 1) * groups] = part.reshape((groups,) + g_send.shape[1:]).astype(BF16)
+
+    def scatter(k):
+        goal = (me + k) % n_all
+        return pltpu.make_async_remote_copy(
+            src_ref=g_send.at[goal], dst_ref=g_recv.at[k - 1],
+            send_sem=g_s.at[k - 1], recv_sem=g_r.at[k - 1],
+            device_id=(goal // n_col, goal % n_col), device_id_type=MESH,
+        )
+
+    def gather(k):
+        goal = (me + k) % n_all
+        return pltpu.make_async_remote_copy(
+            src_ref=grad_ref.at[me], dst_ref=grad_ref.at[me],
+            send_sem=h_s.at[k - 1], recv_sem=h_r.at[k - 1],
+            device_id=(goal // n_col, goal % n_col), device_id_type=MESH,
+        )
+
+    for k in range(1, n_all):
+        scatter(k).start()
     adjoint_ref[...] = adjoint
-    total = g_send[place].astype(F32)
-    for e in range(1, plane):
-        g_copies[e - 1].wait_recv()
-        total = total + g_recv[e - 1].astype(F32)
-    s_all[z] = total.astype(BF16)
-    h_copies = [
-        send(s_all.at[z], s_all.at[z], h_s.at[d - 1], h_r.at[d - 1], z_peer(d))
-        for d in range(1, n_z)
-    ]
-    for copy in h_copies:
-        copy.wait_recv()
-    total = s_all[0].astype(F32)
-    for d in range(1, n_z):
-        total = total + s_all[d].astype(F32)
-    grad_ref[place] = (total * factor).astype(BF16)
-    i_copies = [
-        send(grad_ref.at[place], grad_ref.at[place], i_s.at[e - 1], i_r.at[e - 1], plane_peer(e)[1])
-        for e in range(1, plane)
-    ]
-    for copy in i_copies:
-        copy.wait_recv()
-    started += g_copies + h_copies + i_copies
+    total = g_send[me].astype(F32)
+    for k in range(1, n_all):
+        scatter(k).wait_recv()
+        total = total + g_recv[k - 1].astype(F32)
+    grad_ref[me] = (total * factor).astype(BF16)
+    for k in range(1, n_all):
+        gather(k).start()
+    for k in range(1, n_all):
+        gather(k).wait_recv()
+    for k in range(1, n_all):
+        scatter(k).wait_send()
+        gather(k).wait_send()
     for copy in started:
         copy.wait_send()
 
@@ -258,21 +263,28 @@
 def finish(states_in, adjoint_in, grads_in, states_out, adjoint_out, weight_out, input_out):
     states_out[...] = states_in[...]
     adjoint_out[...] = adjoint_in[...]
-    grads = grads_in[...].astype(F32).reshape(-1, grads_in.shape[2])
-    weight_out[...] = grads[: weight_out.shape[0]]
-    input_out[...] = grads[weight_out.shape[0] :]
+    rows, width = weight_out.shape
+    halves = width // LANES
+    groups = grads_in.shape[0] // halves
+    for h in range(halves):
+        part = grads_in[h * groups : (h + 1) * groups].astype(F32).reshape(-1, LANES)
+        at = pl.ds(h * LANES, LANES)
+        weight_out[:, at] = part[:rows]
+        input_out[:, at] = part[rows:]
 
 
 def fits(n_row, n_col, nodes, width, inputs, slots, block):
     plan = 4 * slots * block * block * (n_row + n_col)
     plan += 8 * nodes * width * (n_row + n_col)
-    plane = 2 * n_col
+    groups = n_row * n_col // max(width // LANES, 1)
     return (
         plan <= VMEM_PLAN
         and nodes == block
         and width % nodes == 0
         and n_row % 2 == 0
-        and (width + inputs) % (16 * plane) == 0
+        and width % LANES == 0
+        and groups * (width // LANES) == n_row * n_col
+        and (width + inputs) % (SUBLANES * groups) == 0
     )
 
 
@@ -281,12 +293,12 @@
     tile_rows, tile_cols, tile_live, weight, input_map,
 ):
     n_row, n_col = lax.axis_size("row"), lax.axis_size("col")
-    n_z, plane = n_row // 2, 2 * n_col
+    n_z, n_all = n_row // 2, n_row * n_col
     nodes, width = starting_state.shape
     inputs = features.shape[1]
     slots, block = tile_values.shape[2], tile_values.shape[3]
     factor = 1.0 / math.sqrt(nodes * n_row * n_col)
-    rows_each = (width + inputs) // plane
+    shard = ((width + inputs) * width // LANES // n_all, LANES)
     vmem = pl.BlockSpec(memory_space=pltpu.VMEM)
     hbm = pl.BlockSpec(memory_space=pltpu.HBM)
     operands = (
@@ -299,14 +311,14 @@
     ]
     piece = (nodes, width)
     sems = []
-    for count in (n_col - 1, n_z, n_z - 1, n_z - 1, n_z, n_col - 1, plane - 1, n_z - 1, plane - 1):
+    for count in (n_col - 1, n_z, n_z - 1, n_z - 1, n_z, n_col - 1, n_all - 1, n_all - 1):
         sems += [pltpu.SemaphoreType.DMA((count,)), pltpu.SemaphoreType.DMA((count,))]
     states, adjoint, grads = pl.pallas_call(
         functools.partial(kernel, n_row, n_col, factor),
         out_shape=(
             jax.ShapeDtypeStruct(piece, F32),
             jax.ShapeDtypeStruct(piece, F32),
-            jax.ShapeDtypeStruct((plane, rows_each, width), BF16),
+            jax.ShapeDtypeStruct((n_all,) + shard, BF16),
         ),
         in_specs=[hbm] * len(operands),
         out_specs=(vmem, vmem, vmem),
@@ -322,9 +334,8 @@
             pltpu.VMEM((n_row,) + piece, BF16),
             pltpu.VMEM((n_col - 1,) + piece, BF16),
             pltpu.VMEM((n_col - 1,) + piece, BF16),
-            pltpu.VMEM((plane, rows_each, width), BF16),
-            pltpu.VMEM((plane - 1, rows_each, width), BF16),
-            pltpu.VMEM((n_z, rows_each, width), BF16),
+            pltpu.VMEM((n_all,) + shard, BF16),
+            pltpu.VMEM((n_all - 1,) + shard, BF16),
         ] + sems,
         compiler_params=pltpu.CompilerParams(
             collective_id=0, has_side_effects=True, vmem_limit_bytes=KERNEL_LIMIT

time: 48.5 us -> 50.6 us (1.043)
  Pallas kernels: 47.7 us -> 49.8 us
    pallas_call x1, Pallas kernels: 46.8 us -> 48.9 us  [kernel_path(): pl.pallas_call(functools.partial(kernel, n_row, n_col, factor), out_shape...]
where the time goes in v3:
time: 50.6 us; the launch traced here: 50.4 us
  Pallas kernels  49.8 us (98%)
  between operations  0.64 us (1%)
    pallas_call x1, Pallas kernels, kernel_path(): pl.pallas_call(functools.partial(kernel, n_row, n_col, factor), out_shape...  48.9 us

profile of v3, /device:TPU:0, one launch (start us, length us, event | category | flops | bytes accessed | tf_op | source)
XLA Modules:
  0.0 50.4 jit_solution(9628394677184645512)
XLA Ops:
  0.6 48.9 %graph_window.1 = (f32[128,256]{1,0:T(8,128)S(1)}, f32[128,256]{1,0:T(8,128)S(1)}, bf16[32,24,128]{2,1,0:T(8,128)(2,1)S(1)}) custom-call(f32[128,256]{1,0:T(8,128)} %state_in.1, f32[128,128]{1,0:T(8,128)} %feat_in.1, f32[128,256]{1,0:T(8,128)} %cot_in.1, s32[1,128]{1,0:T(1,128)} %bitcast.1, bf16[1,1,4,128,128]{4,3,2,1,0:T(8,128)(2,1)} %val_in.1, ...), custom_call_target="tpu_custom_call" | custom-call | tf_op jit(solution)/shard_map/graph_window/pallas_call | solution.py:316
  49.6 0.9 %finish.1 = (f32[128,256]{1,0:T(8,128)}, f32[128,256]{1,0:T(8,128)}, f32[256,256]{1,0:T(8,128)}, f32[128,256]{1,0:T(8,128)}) custom-call(f32[128,256]{1,0:T(8,128)S(1)} %get-tuple-element.7.states_in, f32[128,256]{1,0:T(8,128)S(1)} %get-tuple-element.8.adjoint_in, bf16[32,24,128]{2,1,0:T(8,128)(2,1)S(1)} %get-tuple-element.9.grads_in), custom_call_target="tpu_custom_call" | custom-call | tf_op jit(solution)/shard_map/finish/pallas_call | solution.py:345

commit v4 on v2

--- a/solution.py
+++ b/solution.py
@@ -69,24 +69,18 @@
     states_ref, adjoint_ref, grad_ref,
     state_ref, feat_ref, cot_ref, deg_ref, val_ref, rows_ref, cols_ref, live_ref, w_ref, map_ref, in_sem,
     fwd_l, adj_l, gath, core_send, core_recv, z_send, z_recv, gath2, q_send, q_recv,
-    g_send, g_recv, s_all,
-    a_s, a_r, b_s, b_r, c_s, c_r, d_s, d_r, e_s, e_r, f_s, f_r, g_s, g_r, h_s, h_r, i_s, i_r,
+    both_t, gx_send, gx_recv, g_send, g_recv, s_all,
+    a_s, a_r, b_s, b_r, c_s, c_r, d_s, d_r, e_s, e_r, f_s, f_r, g_s, g_r, h_s, h_r, i_s, i_r, gx_s, gx_r, j_s, j_r,
 ):
     r, c = lax.axis_index("row"), lax.axis_index("col")
     n_z = n_row // 2
-    plane = 2 * n_col
     z, core = r // 2, r % 2
     other = 1 - core
     nodes, width = state_ref.shape
     slots, block = val_ref.shape[2], val_ref.shape[3]
-    place = c * 2 + core
 
     def z_peer(d):
         return (2 * ((z + d) % n_z) + core, c)
-
-    def plane_peer(e):
-        p = (place + e) % plane
-        return p, (2 * z + p % 2, p // 2)
 
     def send(src, dst, s_sem, r_sem, device):
         copy = pltpu.make_async_remote_copy(
@@ -101,8 +95,9 @@
     barrier = pltpu.get_barrier_semaphore()
     for d in range(1, n_z):
         pl.semaphore_signal(barrier, inc=1, device_id=z_peer(d), device_id_type=MESH)
-    for e in range(1, plane):
-        pl.semaphore_signal(barrier, inc=1, device_id=plane_peer(e)[1], device_id_type=MESH)
+    for d in range(1, n_col):
+        pl.semaphore_signal(barrier, inc=1, device_id=(r, (c + d) % n_col), device_id_type=MESH)
+    pl.semaphore_signal(barrier, inc=1, device_id=(2 * z + other, c), device_id_type=MESH)
 
     pairs = (
         (deg_in, deg_ref), (state_in, state_ref), (rows_in, rows_ref), (cols_in, cols_ref),
@@ -122,7 +117,7 @@
     inv = jnp.concatenate([inv] * (width // nodes), axis=1)
     gath[c] = (inv * state_ref[...]).astype(BF16)
 
-    pl.semaphore_wait(barrier, n_z - 1 + plane - 1)
+    pl.semaphore_wait(barrier, n_z - 1 + n_col - 1 + 1)
 
     a_copies = []
     for d in range(1, n_col):
@@ -154,27 +149,27 @@
     started += a_copies
 
     picked = jnp.concatenate([gath[rows_ref[0, 0, t]] for t in range(slots)], axis=0)
-    order = list(range(1, n_z)) + [0]
+    order = sorted(range(1, n_z), key=lambda d: -min(d, n_z - d)) + [0]
     b_copies = {}
     for d in order:
         core_send[d] = jnp.dot(fwd_l[0, d], picked, preferred_element_type=F32).astype(BF16)
         b_copies[d] = send(
             core_send.at[d], core_recv.at[d], b_s.at[d], b_r.at[d], (2 * z + other, c)
         )
-    c_copies = []
+    c_copies = {}
     for d in order:
         mine = jnp.dot(fwd_l[1, d], picked, preferred_element_type=F32)
         b_copies[d].wait_recv()
         total = mine + core_recv[d].astype(F32)
         if d:
             z_send[d - 1] = total.astype(BF16)
-            c_copies.append(
-                send(z_send.at[d - 1], z_recv.at[d - 1], c_s.at[d - 1], c_r.at[d - 1], z_peer(d))
+            c_copies[d] = send(
+                z_send.at[d - 1], z_recv.at[d - 1], c_s.at[d - 1], c_r.at[d - 1], z_peer(d)
             )
-    for d in range(1, n_z):
-        c_copies[d - 1].wait_recv()
+    for d in reversed(order[:-1]):
+        c_copies[d].wait_recv()
         total = total + z_recv[d - 1].astype(F32)
-    started += list(b_copies.values()) + c_copies
+    started += list(b_copies.values()) + list(c_copies.values())
 
     summed = inv * total
     states = jnp.tanh(
@@ -190,7 +185,7 @@
     ]
     e_copies = [send(gath2.at[r], gath2.at[r], e_s.at[0], e_r.at[0], (2 * z + other, c))]
     states_ref[...] = states
-    both_t = jnp.concatenate([summed.T, feat.T], axis=0).astype(BF16)
+    both_t[...] = jnp.concatenate([summed.T, feat.T], axis=0).reshape(both_t.shape).astype(BF16)
     for d in range(1, n_z):
         d_copies[d - 1].wait_recv()
         slot = 2 * ((z + n_z - d) % n_z) + core
@@ -220,19 +215,24 @@
     )
     masked = (slopes * adjoint).astype(BF16)
 
-    grad = jnp.dot(both_t, masked, preferred_element_type=F32)
-    g_send[...] = grad.reshape(g_send.shape).astype(BF16)
+    gx_send[...] = (
+        jnp.dot(both_t[other], masked, preferred_element_type=F32).reshape(gx_send.shape).astype(BF16)
+    )
+    gx_copy = send(gx_send, gx_recv, gx_s.at[0], gx_r.at[0], (2 * z + other, c))
+    grad = jnp.dot(both_t[core], masked, preferred_element_type=F32).reshape(g_send.shape)
+    adjoint_ref[...] = adjoint
+    gx_copy.wait_recv()
+    g_send[...] = (grad + gx_recv[...].astype(F32)).astype(BF16)
     g_copies = []
-    for e in range(1, plane):
-        p, device = plane_peer(e)
+    for d in range(1, n_col):
+        goal = (c + d) % n_col
         g_copies.append(
-            send(g_send.at[p], g_recv.at[e - 1], g_s.at[e - 1], g_r.at[e - 1], device)
-        )
-    adjoint_ref[...] = adjoint
-    total = g_send[place].astype(F32)
-    for e in range(1, plane):
-        g_copies[e - 1].wait_recv()
-        total = total + g_recv[e - 1].astype(F32)
+            send(g_send.at[goal], g_recv.at[d - 1], g_s.at[d - 1], g_r.at[d - 1], (r, goal))
+        )
+    total = g_send[c].astype(F32)
+    for d in range(1, n_col):
+        g_copies[d - 1].wait_recv()
+        total = total + g_recv[d - 1].astype(F32)
     s_all[z] = total.astype(BF16)
     h_copies = [
         send(s_all.at[z], s_all.at[z], h_s.at[d - 1], h_r.at[d - 1], z_peer(d))
@@ -243,14 +243,25 @@
     total = s_all[0].astype(F32)
     for d in range(1, n_z):
         total = total + s_all[d].astype(F32)
-    grad_ref[place] = (total * factor).astype(BF16)
+    mine = core * n_col + c
+    grad_ref[mine] = (total * factor).astype(BF16)
+
     i_copies = [
-        send(grad_ref.at[place], grad_ref.at[place], i_s.at[e - 1], i_r.at[e - 1], plane_peer(e)[1])
-        for e in range(1, plane)
-    ]
-    for copy in i_copies:
+        send(grad_ref.at[mine], grad_ref.at[mine], i_s.at[d - 1], i_r.at[d - 1], (r, (c + d) % n_col))
+        for d in range(1, n_col)
+    ]
+    j_copies = [
+        send(grad_ref.at[mine], grad_ref.at[mine], j_s.at[0], j_r.at[0], (2 * z + other, c))
+    ]
+    for d in range(1, n_col):
+        i_copies[d - 1].wait_recv()
+        slot = core * n_col + (c + n_col - d) % n_col
+        j_copies.append(
+            send(grad_ref.at[slot], grad_ref.at[slot], j_s.at[d], j_r.at[d], (2 * z + other, c))
+        )
+    for copy in j_copies:
         copy.wait_recv()
-    started += g_copies + h_copies + i_copies
+    started += [gx_copy] + g_copies + h_copies + i_copies + j_copies
     for copy in started:
         copy.wait_send()
 
@@ -299,7 +310,7 @@
     ]
     piece = (nodes, width)
     sems = []
-    for count in (n_col - 1, n_z, n_z - 1, n_z - 1, n_z, n_col - 1, plane - 1, n_z - 1, plane - 1):
+    for count in (n_col - 1, n_z, n_z - 1, n_z - 1, n_z, n_col - 1, n_col - 1, n_z - 1, n_col - 1, 1, n_col):
         sems += [pltpu.SemaphoreType.DMA((count,)), pltpu.SemaphoreType.DMA((count,))]
     states, adjoint, grads = pl.pallas_call(
         functools.partial(kernel, n_row, n_col, factor),
@@ -322,8 +333,11 @@
             pltpu.VMEM((n_row,) + piece, BF16),
             pltpu.VMEM((n_col - 1,) + piece, BF16),
             pltpu.VMEM((n_col - 1,) + piece, BF16),
-            pltpu.VMEM((plane, rows_each, width), BF16),
-            pltpu.VMEM((plane - 1, rows_each, width), BF16),
+            pltpu.VMEM((2, (width + inputs) // 2, nodes), BF16),
+            pltpu.VMEM((n_col, rows_each, width), BF16),
+            pltpu.VMEM((n_col, rows_each, width), BF16),
+            pltpu.VMEM((n_col, rows_each, width), BF16),
+            pltpu.VMEM((n_col - 1, rows_each, width), BF16),
             pltpu.VMEM((n_z, rows_each, width), BF16),
         ] + sems,
         compiler_params=pltpu.CompilerParams(

time: 48.5 us -> 48.4 us (level)
  no operation moved by 1% of the time
where the time goes in v4:
time: 48.4 us; the launch traced here: 48.2 us
  Pallas kernels  47.6 us (98%)
  between operations  0.64 us (1%)
    pallas_call x1, Pallas kernels, kernel_path(): pl.pallas_call(functools.partial(kernel, n_row, n_col, factor), out_shape...  46.7 us

profile of v4, /device:TPU:0, one launch (start us, length us, event | category | flops | bytes accessed | tf_op | source)
XLA Modules:
  0.0 48.2 jit_solution(17163801502942051084)
XLA Ops:
  0.6 46.7 %graph_window.1 = (f32[128,256]{1,0:T(8,128)S(1)}, f32[128,256]{1,0:T(8,128)S(1)}, bf16[8,48,256]{2,1,0:T(8,128)(2,1)S(1)}) custom-call(f32[128,256]{1,0:T(8,128)} %state_in.1, f32[128,128]{1,0:T(8,128)} %feat_in.1, f32[128,256]{1,0:T(8,128)} %cot_in.1, s32[1,128]{1,0:T(1,128)} %bitcast.1, bf16[1,1,4,128,128]{4,3,2,1,0:T(8,128)(2,1)} %val_in.1, ...), custom_call_target="tpu_custom_call" | custom-call | tf_op jit(solution)/shard_map/graph_window/pallas_call | solution.py:315
  47.4 0.9 %finish.1 = (f32[128,256]{1,0:T(8,128)}, f32[128,256]{1,0:T(8,128)}, f32[256,256]{1,0:T(8,128)}, f32[128,256]{1,0:T(8,128)}) custom-call(f32[128,256]{1,0:T(8,128)S(1)} %get-tuple-element.7.states_in, f32[128,256]{1,0:T(8,128)S(1)} %get-tuple-element.8.adjoint_in, bf16[8,48,256]{2,1,0:T(8,128)(2,1)S(1)} %get-tuple-element.9.grads_in), custom_call_target="tpu_custom_call" | custom-call | tf_op jit(solution)/shard_map/finish/pallas_call | solution.py:348
